TPU v7x, 32 devices: a whole 2x2x4 slice. The times are simulated.
32 devices in a mesh: dom: 16 (over z, x, core), cell: 2 (over y).
Axes of the slice: x: 2, y: 2, z: 4, core: 2. Of those that a mesh axis runs over, the one named last changes fastest.
Arguments:
- models: bfloat16 [2, 512, 4096], P(None, 'dom', 'cell'), may hold values from -12 to 12
- gradients: bfloat16 [2, 512, 4096], P(None, 'dom', 'cell'), may hold values from -48 to 48
- length_scale: float32 [1], replicated, may hold values from 3 to 12
Outputs:
- update: float32 [2, 512, 4096], P(None, 'dom', 'cell')
All inputs are finite; a program needn't handle non-finite values.
Results may differ from a plain program's by a relative error of at most 0.00045.
The roundings to bfloat16 on the way count: a program that leaves them out, or rounds other values in their place, can miss the bound.
Values may be sent and summed in bfloat16 or wider, within the bound.
A program may use at most 64 MiB of HBM per device.

v0:
```python
import jax
import jax.numpy as jnp
from jax import lax
from jax.sharding import PartitionSpec as P


def body(models, gradients, length_scale):
    local_models, local_grads = (
        lax.all_to_all(models, "dom", split_axis=2, concat_axis=1, tiled=True),
        lax.all_to_all(gradients, "dom", split_axis=2, concat_axis=1, tiled=True),
    )
    cell_block = local_models.shape[2]
    particles = local_models.shape[1]
    cell_count = cell_block * lax.axis_size("dom") * lax.axis_size("cell")
    scale_value = length_scale[0]
    divisor = scale_value * cell_count
    partial_value = jnp.einsum(
        "kpc,kqc->pq", local_models, local_models, preferred_element_type=jnp.float32
    )
    summed = lax.psum(partial_value, "cell")
    row_block = lax.psum_scatter(summed, "dom", scatter_dimension=0, tiled=True)
    row_count = row_block.shape[0]
    row_start = lax.axis_index("dom") * row_count
    own_squares = jnp.diagonal(lax.dynamic_slice_in_dim(row_block, row_start, row_count, 1))
    squares = lax.all_gather(own_squares, "dom", axis=0, tiled=True)
    distance = own_squares[:, None] + squares[None, :] - 2.0 * row_block
    kernel = lax.all_gather(
        jnp.exp(-distance / divisor).astype(jnp.bfloat16), "dom", axis=0, tiled=True
    )
    rowsum = jnp.sum(kernel.astype(jnp.float32), axis=1)
    stacked = jnp.concatenate((local_grads, local_models), axis=2)
    product = jnp.einsum("pq,kqc->kpc", kernel, stacked, preferred_element_type=jnp.float32)
    attract = product[:, :, :cell_block]
    pulled = product[:, :, cell_block:]
    update = (
        attract
        + 2.0 / scale_value * (rowsum[None, :, None] * local_models.astype(jnp.float32) - pulled)
    ) / particles
    return lax.all_to_all(update, "dom", split_axis=1, concat_axis=2, tiled=True)


def solution(mesh):
    placed = (P(None, "dom", "cell"), P(None, "dom", "cell"), P())
    return jax.shard_map(
        body, mesh=mesh, in_specs=placed, out_specs=P(None, "dom", "cell"), check_vma=False
    )
```

profile of v0, /device:TPU:0, one launch (start us, length us, event | category | flops | bytes accessed | tf_op | source)
XLA Modules:
  0.0 188.0 jit_solution(7006938158542495927)
XLA Ops:
  6.5 2.2 %copy.16 = bf16[2,32,2048]{1,0,2:T(2,128)(2,1)S(1)} copy(bf16[2,32,2048]{2,1,0:T(8,128)(2,1)} %param.3) | data formatting | bytes 524288 | tf_op args[0]
  8.8 1.0 reshape.20
  9.7 17.2 %all_to_all.54 = bf16[16,2,4096]{2,1,0:T(2,128)(2,1)S(1)} all-to-all(bf16[16,2,4096]{2,1,0:T(2,128)(2,1)S(1)} %reshape.20), channel_id=1, replica_groups=mesh['dom'=16,'cell'=2] {'dom'}, dimensions={0} | all-to-all | bytes 524288 | tf_op jit(solution)/shard_map/all_to_all | solution.py:9
  26.9 0.5 reshape.21
  27.4 0.7 copy.17
  28.2 1.3 convolution_bitcast_fusion
  29.5 0.0 reduce-scatter.2.cloned.1.call-update
  29.5 0.9 copy-done
  30.4 0.7 copy.14
  31.2 1.7 reshape.22
  32.9 3.5 %all-to-all-start = ((bf16[16,2,4096]{2,1,0:T(2,128)(2,1)}), bf16[16,2,4096]{2,1,0:T(2,128)(2,1)S(1)}, u32[]{:S(2)}, u32[]{:S(2)}) async-start(bf16[16,2,4096]{2,1,0:T(2,128)(2,1)} %reshape.22), calls=%async_computation | async-start | bytes 524288 | tf_op jit(solution)/shard_map/all_to_all | solution.py:10
  36.4 0.0 all-reduce.3.cloned.1.call-start
  37.2 0.6 copy-done.2
  37.8 0.6 dynamic-slice
  39.1 46.5 %reduce-scatter.2.cloned.1.call-done = f32[32,512]{1,0:T(8,128)} async-done(((f32[512,512]{1,0:T(8,128)}), f32[32,512]{1,0:T(8,128)}) %reduce-scatter.2.cloned.1.call-update) | async-done | bytes 65552 | tf_op jit(solution)/shard_map/reduce_scatter | solution.py:21
  85.6 0.0 all-reduce.3.cloned.1.call-update
  85.6 0.5 reshape.23
  86.1 0.7 copy.15
  86.8 20.9 %all-reduce.3.cloned.1.call-done = f32[32,512]{1,0:T(8,128)} async-done(((f32[32,512]{1,0:T(8,128)}), f32[32,512]{1,0:T(8,128)}) %all-reduce.3.cloned.1.call-update) | async-done | bytes 65552 | tf_op jit(solution)/shard_map/psum | solution.py:20
  107.8 0.8 constant_dynamic-slice_fusion
  108.6 0.7 gather_fusion
  109.3 0.2 dynamic-update-slice
  109.5 32.7 %all-reduce = f32[512]{0:T(512)S(1)} all-reduce(f32[512]{0:T(512)S(1)} %dynamic-update-slice), channel_id=1, replica_groups=mesh['dom'=16,'cell'=2] {'dom'}, use_global_device_ids=true, to_apply=%add | all-reduce | flops 512 | bytes 4096
  142.2 0.1 exponential_convert_fusion
  142.3 18.7 %all_gather.7 = bf16[512,512]{1,0:T(8,128)(2,1)S(1)} all-gather(bf16[32,512]{1,0:T(8,128)(2,1)S(1)} %exponential_convert_fusion), channel_id=1, replica_groups=mesh['dom'=16,'cell'=2] {'dom'}, dimensions={0}, use_global_device_ids=true | all-gather | bytes 557056 | tf_op jit(solution)/shard_map/all_gather | solution.py:27
  161.0 0.1 convert_reduce_fusion
  161.1 0.4 convolution_bitcast_fusion.1
  161.6 0.2 fusion.2
  161.8 0.4 copy.20
  162.2 17.8 %all_to_all.55 = f32[2,512,128]{2,0,1:T(2,128)S(1)} all-to-all(f32[2,512,128]{2,0,1:T(2,128)S(1)} %copy.20), channel_id=1, replica_groups=mesh['dom'=16,'cell'=2] {'dom'}, dimensions={1} | all-to-all | bytes 1048576 | tf_op jit(solution)/shard_map/all_to_all | solution.py:39
  180.0 0.3 copy.21
  180.3 0.9 all_to_all.50
  (8 shorter events, 0.0 us)
Async XLA Ops:
  6.5 79.0 %reduce-scatter.2.cloned.1.call-start = ((), (), s32[]{:S(2)}) async-start(), calls=%async_computation.4 | async-start | bytes 1114112 | tf_op jit(solution)/shard_map/reduce_scatter | solution.py:21
  29.5 0.9 copy-start
  32.9 52.7 %all-to-all-start = ((bf16[16,2,4096]{2,1,0:T(2,128)(2,1)}), bf16[16,2,4096]{2,1,0:T(2,128)(2,1)S(1)}, u32[]{:S(2)}, u32[]{:S(2)}) async-start(bf16[16,2,4096]{2,1,0:T(2,128)(2,1)} %reshape.22), calls=%async_computation | async-start | bytes 524288 | tf_op jit(solution)/shard_map/all_to_all | solution.py:10
  36.4 71.4 %all-reduce.3.cloned.1.call-start = ((), (), s32[]{:S(2)}) async-start(), calls=%async_computation.5 | async-start | bytes 131072 | tf_op jit(solution)/shard_map/psum | solution.py:20
  37.1 0.7 copy-start.2
  108.5 33.6 %copy-start.1 = (f32[32,512]{1,0:T(8,128)S(1)}, f32[32,512]{1,0:T(8,128)}, u32[]{:S(2)}) copy-start(f32[32,512]{1,0:T(8,128)} %all-reduce.3.cloned.1.call-done) | copy-start | bytes 196612
Sparse Core Ops, SparseCore 0:
  29.6 55.8 reduce-scatter.1
  87.8 19.9 all-reduce.2
where the time goes:
time: 188 us
  blocking collectives  86.4 us (46%)
  waiting for transfers between devices  67.4 us (36%)
  between operations  14.8 us (8%)
  local copies, waits for them, and re-layouts  13.6 us (7%)
  starting transfers between devices  3.58 us (2%)
    reduce_scatter x1, waiting for transfers between devices, body(): row_block = lax.psum_scatter(summed, 'dom', scatter_dimension=0, tiled=True)  46.5 us
    unnamed x1, blocking collectives  32.7 us
    psum x1, waiting for transfers between devices, body(): summed = lax.psum(partial_value, 'cell')  20.9 us
    all_gather x1, blocking collectives, body(): lax.all_gather(jnp.exp(-distance / divisor).astype(jnp.bfloat16), 'dom',...  18.7 us
    all_to_all x1, blocking collectives, body(): lax.all_to_all(update, 'dom', split_axis=1, concat_axis=2, tiled=True)  17.8 us
    all_to_all x1, blocking collectives, body(): lax.all_to_all(models, 'dom', split_axis=2, concat_axis=1, tiled=True)  17.2 us
    unnamed x15, local copies, waits for them, and re-layouts  9.06 us
  transfers between devices with their start and end apart: 3, of which 2 were waited for; matrix products, arithmetic and copies ran while one was open for 2% of the time, Pallas kernels for 0%

commit v1 on v0

--- a/solution.py
+++ b/solution.py
@@ -1,10 +1,17 @@
+import functools
+import math
+
 import jax
 import jax.numpy as jnp
 from jax import lax
+from jax.experimental import pallas as pl
+from jax.experimental.pallas import tpu as pltpu
 from jax.sharding import PartitionSpec as P
 
-
-def body(models, gradients, length_scale):
+MESH = pl.DeviceIdType.MESH
+
+
+def plain_body(models, gradients, length_scale):
     local_models, local_grads = (
         lax.all_to_all(models, "dom", split_axis=2, concat_axis=1, tiled=True),
         lax.all_to_all(gradients, "dom", split_axis=2, concat_axis=1, tiled=True),
@@ -39,7 +46,323 @@
     return lax.all_to_all(update, "dom", split_axis=1, concat_axis=2, tiled=True)
 
 
+def stein_kernel(
+    layers, group, planes,
+    scale_ref, models_ref, grads_ref, out_ref,
+    m_all, g_all, part, inbox, krows, base, outbox,
+    local_sem, a2a_send, m_recv, g_recv, fwd_send,
+    rs_send, rs_recv, k_send, k_recv, o_send, o_recv,
+):
+    fields, rows, width = models_ref.shape
+    cells = width // group
+    slab = group * rows
+    count = layers * slab
+    peers = group * planes
+    piece = slab // peers
+    total_cells = width * planes
+    dom = lax.axis_index("dom")
+    y = lax.axis_index("cell")
+    z = dom // group
+    g = dom % group
+    me = g * planes + y
+    has_up = z + 1 < layers
+    has_down = z > 0
+
+    def columns(which):
+        return pl.ds(pl.multiple_of(which * cells, 128), cells)
+
+    def layer_id(which):
+        return (z * group + which // planes, which % planes)
+
+    barrier = pltpu.get_barrier_semaphore()
+    for k in range(1, peers):
+        pl.semaphore_signal(
+            barrier, inc=1, device_id=layer_id((me + k) % peers), device_id_type=MESH
+        )
+
+    @pl.when(has_up)
+    def _():
+        pl.semaphore_signal(barrier, inc=1, device_id=(dom + group, y), device_id_type=MESH)
+
+    @pl.when(has_down)
+    def _():
+        pl.semaphore_signal(barrier, inc=1, device_id=(dom - group, y), device_id_type=MESH)
+
+    tensors = ((models_ref, m_all, m_recv), (grads_ref, g_all, g_recv))
+    locals_ = []
+    for t, (src, dst, _) in enumerate(tensors):
+        copy = pltpu.make_async_copy(
+            src.at[:, :, columns(g)], dst.at[z, g], local_sem.at[t]
+        )
+        copy.start()
+        locals_.append(copy)
+
+    neighbours = jnp.where(has_up, 1, 0) + jnp.where(has_down, 1, 0)
+    pl.semaphore_wait(barrier, peers - 1 + neighbours)
+
+    pending = []
+    for t, (src, dst, recv) in enumerate(tensors):
+        for k in range(1, group):
+            to = (g + k) % group
+            copy = pltpu.make_async_remote_copy(
+                src_ref=src.at[:, :, columns(to)],
+                dst_ref=dst.at[z, g],
+                send_sem=a2a_send.at[t, k],
+                recv_sem=recv.at[z, g],
+                device_id=(z * group + to, y),
+                device_id_type=MESH,
+            )
+            copy.start()
+            pending.append(copy)
+
+    def hop(t, up, level, which, step, k):
+        _, buf, recv = tensors[t]
+        return pltpu.make_async_remote_copy(
+            src_ref=buf.at[level, which],
+            dst_ref=buf.at[level, which],
+            send_sem=fwd_send.at[t, up, step, k],
+            recv_sem=recv.at[level, which],
+            device_id=(dom + group if up else dom - group, y),
+            device_id_type=MESH,
+        )
+
+    def chain_step(t, step):
+        for k in range(group):
+            which = (g + group - k) % group
+            if step == 0:
+                if k == 0:
+                    locals_[t].wait()
+                else:
+                    hop(t, 1, z, which, step, k).wait_recv()
+
+                @pl.when(has_up)
+                def _():
+                    hop(t, 1, z, which, step, k).start()
+
+                @pl.when(has_down)
+                def _():
+                    hop(t, 0, z, which, step, k).start()
+
+                continue
+
+            @pl.when(z >= step)
+            def _():
+                hop(t, 1, z - step, which, step, k).wait_recv()
+
+                @pl.when(has_up)
+                def _():
+                    hop(t, 1, z - step, which, step, k).start()
+
+            @pl.when(z + step < layers)
+            def _():
+                hop(t, 0, z + step, which, step, k).wait_recv()
+
+                @pl.when(has_down)
+                def _():
+                    hop(t, 0, z + step, which, step, k).start()
+
+    def chain_drain(t):
+        for step in range(layers):
+            for k in range(group):
+                which = (g + group - k) % group
+
+                @pl.when(jnp.logical_and(z >= step, has_up))
+                def _():
+                    hop(t, 1, z - step, which, step, k).wait_send()
+
+                @pl.when(jnp.logical_and(z + step < layers, has_down))
+                def _():
+                    hop(t, 0, z + step, which, step, k).wait_send()
+
+    def whole(buf, field):
+        return buf[:, :, field].reshape(count, cells)
+
+    for step in range(layers):
+        chain_step(0, step)
+    chain_step(1, 0)
+
+    contract = (((1,), (1,)), ((), ()))
+    gram = jnp.zeros((slab, count), jnp.float32)
+    squares = jnp.zeros((8, count), jnp.float32)
+    ones = jnp.ones((8, cells), jnp.bfloat16)
+    for field in range(fields):
+        every = whole(m_all, field)
+        own = m_all[z, :, field].reshape(slab, cells)
+        gram += lax.dot_general(own, every, contract, preferred_element_type=jnp.float32)
+        wide = every.astype(jnp.float32)
+        wide = wide * wide
+        high = wide.astype(jnp.bfloat16)
+        low = (wide - high.astype(jnp.float32)).astype(jnp.bfloat16)
+        squares += lax.dot_general(ones, high, contract, preferred_element_type=jnp.float32)
+        squares += lax.dot_general(ones, low, contract, preferred_element_type=jnp.float32)
+    part[:, :piece, :] = gram.reshape(peers, piece, count)
+    part[:, piece:, :] = jnp.broadcast_to(squares[None], (peers, 8, count))
+
+    for k in range(1, peers):
+        to = (me + k) % peers
+        copy = pltpu.make_async_remote_copy(
+            src_ref=part.at[to],
+            dst_ref=inbox.at[me],
+            send_sem=rs_send.at[k],
+            recv_sem=rs_recv.at[me],
+            device_id=layer_id(to),
+            device_id_type=MESH,
+        )
+        copy.start()
+        pending.append(copy)
+    inbox[me] = part[me]
+
+    if layers > 2:
+        chain_step(1, 1)
+
+    for k in range(1, peers):
+        source = (me + peers - k) % peers
+        pltpu.make_async_remote_copy(
+            src_ref=part.at[source],
+            dst_ref=inbox.at[source],
+            send_sem=rs_send.at[k],
+            recv_sem=rs_recv.at[source],
+            device_id=layer_id(source),
+            device_id_type=MESH,
+        ).wait_recv()
+    summed = inbox[0]
+    for k in range(1, peers):
+        summed = summed + inbox[k]
+    row_gram = summed[:piece]
+    row_squares = summed[piece:piece + 1]
+    first = z * slab + me * piece
+    row_index = lax.broadcasted_iota(jnp.int32, (piece, count), 0) + first
+    col_index = lax.broadcasted_iota(jnp.int32, (piece, count), 1)
+    own_squares = jnp.sum(
+        jnp.where(row_index == col_index, row_gram, 0.0), axis=1, keepdims=True
+    )
+    scale = scale_ref[0]
+    distance = own_squares + row_squares - 2.0 * row_gram
+    divisor = jnp.full((piece, count), scale * total_cells, jnp.float32)
+    krows[me] = jnp.exp(-distance / divisor).astype(jnp.bfloat16)
+
+    for k in range(1, peers):
+        to = (me + k) % peers
+        copy = pltpu.make_async_remote_copy(
+            src_ref=krows.at[me],
+            dst_ref=krows.at[me],
+            send_sem=k_send.at[k],
+            recv_sem=k_recv.at[me],
+            device_id=layer_id(to),
+            device_id_type=MESH,
+        )
+        copy.start()
+        pending.append(copy)
+    for k in range(1, peers):
+        source = (me + peers - k) % peers
+        pltpu.make_async_remote_copy(
+            src_ref=krows.at[source],
+            dst_ref=krows.at[source],
+            send_sem=k_send.at[k],
+            recv_sem=k_recv.at[source],
+            device_id=layer_id(source),
+            device_id_type=MESH,
+        ).wait_recv()
+
+    kernel = krows[...].reshape(slab, count)
+    rowsum = jnp.sum(kernel.astype(jnp.float32), axis=1, keepdims=True)
+    factor = 2.0 / jnp.full((slab, cells), scale, jnp.float32)
+    for field in range(fields):
+        own = m_all[z, :, field].reshape(slab, cells).astype(jnp.float32)
+        pulled = jnp.dot(kernel, whole(m_all, field), preferred_element_type=jnp.float32)
+        base[field] = factor * (rowsum * own - pulled)
+
+    for step in range(2 if layers > 2 else 1, layers):
+        chain_step(1, step)
+
+    def out_copy(field, to, source, k):
+        return pltpu.make_async_remote_copy(
+            src_ref=outbox.at[field, to],
+            dst_ref=out_ref.at[field, :, columns(source)],
+            send_sem=o_send.at[field, k],
+            recv_sem=o_recv.at[field, source],
+            device_id=(z * group + to, y),
+            device_id_type=MESH,
+        )
+
+    for field in range(fields):
+        attract = jnp.dot(kernel, whole(g_all, field), preferred_element_type=jnp.float32)
+        update = (attract + base[field]) * (1.0 / count)
+        outbox[field] = update.reshape(group, rows, cells)
+        for k in range(1, group):
+            copy = out_copy(field, (g + k) % group, g, k)
+            copy.start()
+            pending.append(copy)
+        out_ref[field, :, columns(g)] = outbox[field, g]
+    for field in range(fields):
+        for k in range(1, group):
+            source = (g + group - k) % group
+            out_copy(field, source, source, k).wait_recv()
+    chain_drain(0)
+    chain_drain(1)
+    for copy in pending:
+        copy.wait_send()
+
+
+def fused_body(layers, group, planes, models, gradients, length_scale):
+    fields, rows, width = models.shape
+    cells = width // group
+    slab = group * rows
+    count = layers * slab
+    peers = group * planes
+    piece = slab // peers
+    dma = pltpu.SemaphoreType.DMA
+    return pl.pallas_call(
+        functools.partial(stein_kernel, layers, group, planes),
+        out_shape=jax.ShapeDtypeStruct(models.shape, jnp.float32),
+        in_specs=[
+            pl.BlockSpec(memory_space=pltpu.SMEM),
+            pl.BlockSpec(memory_space=pl.ANY),
+            pl.BlockSpec(memory_space=pl.ANY),
+        ],
+        out_specs=pl.BlockSpec(memory_space=pltpu.VMEM),
+        scratch_shapes=[
+            pltpu.VMEM((layers, group, fields, rows, cells), jnp.bfloat16),
+            pltpu.VMEM((layers, group, fields, rows, cells), jnp.bfloat16),
+            pltpu.VMEM((peers, piece + 8, count), jnp.float32),
+            pltpu.VMEM((peers, piece + 8, count), jnp.float32),
+            pltpu.VMEM((peers, piece, count), jnp.bfloat16),
+            pltpu.VMEM((fields, slab, cells), jnp.float32),
+            pltpu.VMEM((fields, group, rows, cells), jnp.float32),
+            dma((2,)),
+            dma((2, group)),
+            dma((layers, group)),
+            dma((layers, group)),
+            dma((2, 2, layers, group)),
+            dma((peers,)),
+            dma((peers,)),
+            dma((peers,)),
+            dma((peers,)),
+            dma((fields, group)),
+            dma((fields, group)),
+        ],
+        compiler_params=pltpu.CompilerParams(collective_id=0, has_side_effects=True),
+        name="stein",
+    )(length_scale, models, gradients)
+
+
 def solution(mesh):
+    spread, planes = mesh.shape["dom"], mesh.shape["cell"]
+    layers = math.isqrt(spread)
+    group = spread // layers
+
+    def body(models, gradients, length_scale):
+        _, rows, width = models.shape
+        fits = (
+            layers * group == spread
+            and width % (group * 128) == 0
+            and rows % 16 == 0
+            and (group * rows) % (group * planes * 16) == 0
+        )
+        if not fits:
+            return plain_body(models, gradients, length_scale)
+        return fused_body(layers, group, planes, models, gradients, length_scale)
+
     placed = (P(None, "dom", "cell"), P(None, "dom", "cell"), P())
     return jax.shard_map(
         body, mesh=mesh, in_specs=placed, out_specs=P(None, "dom", "cell"), check_vma=False

time: 188 us -> 55.4 us (0.29)
  blocking collectives: 86.4 us -> 0 us
  waiting for transfers between devices: 67.4 us -> 0 us
  Pallas kernels: 0 us -> 52.7 us
  between operations: 14.8 us -> 0.66 us
  local copies, waits for them, and re-layouts: 13.6 us -> 1.87 us
  starting transfers between devices: 3.58 us -> 0 us
    pallas_call x0 -> x1, Pallas kernels: none -> 52.7 us  [fused_body(): pl.pallas_call(functools.partial(stein_kernel, layers, group, planes), ou...]
    reduce_scatter x1 -> x0, waiting for transfers between devices: 46.5 us -> none  [body(): row_block = lax.psum_scatter(summed, 'dom', scatter_dimension=0, tiled=True)]
    all_to_all x2 -> x0, blocking collectives: 35 us -> none  [the longest x1 17.8 us: body(): lax.all_to_all(update, 'dom', split_axis=1, concat_axis=2, tiled=True)]
    unnamed x1 -> x0, blocking collectives: 32.7 us -> none
    psum x1 -> x0, waiting for transfers between devices: 20.9 us -> none  [body(): summed = lax.psum(partial_value, 'cell')]
    all_gather x1 -> x0, blocking collectives: 18.7 us -> none  [body(): lax.all_gather(jnp.exp(-distance / divisor).astype(jnp.bfloat16), 'dom',...]
    unnamed x15 -> x1, local copies, waits for them, and re-layouts: 9.06 us -> 1.87 us
    all_to_all x1 -> x0, starting transfers between devices: 3.53 us -> none  [body(): lax.all_to_all(gradients, 'dom', split_axis=2, concat_axis=1, tiled=True)]
  transfers between devices with their start and end apart: 3 -> 0, of which waited for: 2 -> 0; matrix products, arithmetic and copies ran while one was open for 2% -> 0% of each run, Pallas kernels for 0% -> 0%
where the time goes in v1:
time: 55.4 us; the launch traced here: 55.2 us
  Pallas kernels  52.7 us (95%)
  local copies, waits for them, and re-layouts  1.87 us (3%)
  between operations  0.66 us (1%)
    pallas_call x1, Pallas kernels, fused_body(): pl.pallas_call(functools.partial(stein_kernel, layers, group, planes), ou...  52.7 us
    unnamed x1, local copies, waits for them, and re-layouts  1.87 us

profile of v1, /device:TPU:0, one launch (start us, length us, event | category | flops | bytes accessed | tf_op | source)
XLA Modules:
  0.0 55.2 jit_solution(18252645530107997054)
XLA Ops:
  0.7 52.7 %stein.1 = f32[2,32,2048]{2,1,0:T(8,128)} custom-call(f32[1]{0:T(128)S(6)} %copy.5.scale_ref, bf16[2,32,2048]{2,1,0:T(8,128)(2,1)} %models_ref.1, bf16[2,32,2048]{2,1,0:T(8,128)(2,1)} %grads_ref.1), custom_call_target="tpu_custom_call" | custom-call | tf_op jit(solution)/shard_map/stein/pallas_call | solution.py:315
  53.4 1.9 %copy.6 = f32[2,32,2048]{2,1,0:T(8,128)} copy(f32[2,32,2048]{2,1,0:T(8,128)} %stein.1) | data formatting | bytes 1048576

commit v2 on v1

v2 whole, which is shorter than its diff:
```python
import functools
import math

import jax
import jax.numpy as jnp
from jax import lax
from jax.experimental import pallas as pl
from jax.experimental.pallas import tpu as pltpu
from jax.sharding import PartitionSpec as P

MESH = pl.DeviceIdType.MESH


def plain_body(models, gradients, length_scale):
    local_models, local_grads = (
        lax.all_to_all(models, "dom", split_axis=2, concat_axis=1, tiled=True),
        lax.all_to_all(gradients, "dom", split_axis=2, concat_axis=1, tiled=True),
    )
    cell_block = local_models.shape[2]
    particles = local_models.shape[1]
    cell_count = cell_block * lax.axis_size("dom") * lax.axis_size("cell")
    scale_value = length_scale[0]
    divisor = scale_value * cell_count
    partial_value = jnp.einsum(
        "kpc,kqc->pq", local_models, local_models, preferred_element_type=jnp.float32
    )
    summed = lax.psum(partial_value, "cell")
    row_block = lax.psum_scatter(summed, "dom", scatter_dimension=0, tiled=True)
    row_count = row_block.shape[0]
    row_start = lax.axis_index("dom") * row_count
    own_squares = jnp.diagonal(lax.dynamic_slice_in_dim(row_block, row_start, row_count, 1))
    squares = lax.all_gather(own_squares, "dom", axis=0, tiled=True)
    distance = own_squares[:, None] + squares[None, :] - 2.0 * row_block
    kernel = lax.all_gather(
        jnp.exp(-distance / divisor).astype(jnp.bfloat16), "dom", axis=0, tiled=True
    )
    rowsum = jnp.sum(kernel.astype(jnp.float32), axis=1)
    stacked = jnp.concatenate((local_grads, local_models), axis=2)
    product = jnp.einsum("pq,kqc->kpc", kernel, stacked, preferred_element_type=jnp.float32)
    attract = product[:, :, :cell_block]
    pulled = product[:, :, cell_block:]
    update = (
        attract
        + 2.0 / scale_value * (rowsum[None, :, None] * local_models.astype(jnp.float32) - pulled)
    ) / particles
    return lax.all_to_all(update, "dom", split_axis=1, concat_axis=2, tiled=True)


def stein_kernel(
    layers, group, planes, held,
    scale_ref, models_ref, grads_ref, out_ref,
    m_all, g_all, part, inbox, swap_out, swap_in, krows, base, base_far, outbox, outbox_far,
    local_sem, a2a_send, m_recv, g_recv, fwd_send,
    rs_send, rs_recv, swap_sem, k_send, k_recv, o_send, o_recv,
):
    fields, rows, width = models_ref.shape
    cells = width // group
    slab = group * rows
    count = layers * slab
    peers = group * planes
    piece = slab // peers
    total_cells = width * planes
    spare = cells - held
    near = pl.ds(0, held)
    dom = lax.axis_index("dom")
    y = lax.axis_index("cell")
    z = dom // group
    g = dom % group
    me = g * planes + y
    has_up = z + 1 < layers
    has_down = z > 0
    is_end = jnp.logical_or(z == 0, z == layers - 1)
    is_inner = jnp.logical_and(z > 0, z < layers - 1)
    mate = z + 1 - 2 * (z % 2)
    up_end = z + 1 == layers - 1
    down_end = z - 1 == 0

    def both(left, right):
        return jnp.logical_and(left, right)

    def columns(which, start=0, size=None):
        return pl.ds(pl.multiple_of(which * cells + start, 128), cells if size is None else size)

    def layer_id(which):
        return (z * group + which // planes, which % planes)

    barrier = pltpu.get_barrier_semaphore()
    for k in range(1, peers):
        pl.semaphore_signal(
            barrier, inc=1, device_id=layer_id((me + k) % peers), device_id_type=MESH
        )
    for k in range(1, group):
        pl.semaphore_signal(
            barrier,
            inc=1,
            device_id=(mate * group + (g + k) % group, y),
            device_id_type=MESH,
        )

    @pl.when(has_up)
    def _():
        pl.semaphore_signal(barrier, inc=1, device_id=(dom + group, y), device_id_type=MESH)

    @pl.when(has_down)
    def _():
        pl.semaphore_signal(barrier, inc=1, device_id=(dom - group, y), device_id_type=MESH)

    tensors = ((models_ref, m_all, m_recv), (grads_ref, g_all, g_recv))
    locals_ = []
    for t, (src, dst, _) in enumerate(tensors):
        copy = pltpu.make_async_copy(
            src.at[:, :, columns(g)], dst.at[z, g], local_sem.at[t]
        )
        copy.start()
        locals_.append(copy)

    neighbours = jnp.where(has_up, 1, 0) + jnp.where(has_down, 1, 0)
    pl.semaphore_wait(barrier, peers - 1 + group - 1 + neighbours)

    pending = []
    for t, (src, dst, recv) in enumerate(tensors):
        for k in range(1, group):
            to = (g + k) % group
            copy = pltpu.make_async_remote_copy(
                src_ref=src.at[:, :, columns(to)],
                dst_ref=dst.at[z, g],
                send_sem=a2a_send.at[t, k],
                recv_sem=recv.at[z, g],
                device_id=(z * group + to, y),
                device_id_type=MESH,
            )
            copy.start()
            pending.append(copy)

    def hop(t, up, level, which, step, k, short):
        _, buf, recv = tensors[t]
        block = buf.at[level, which, :, :, near] if short else buf.at[level, which]
        return pltpu.make_async_remote_copy(
            src_ref=block,
            dst_ref=block,
            send_sem=fwd_send.at[t, up, step, k],
            recv_sem=recv.at[level, which],
            device_id=(dom + group if up else dom - group, y),
            device_id_type=MESH,
        )

    def push(t, up, level, which, step, k, verb):
        exists, short = (has_up, up_end) if up else (has_down, down_end)

        @pl.when(both(exists, short))
        def _():
            getattr(hop(t, up, level, which, step, k, True), verb)()

        @pl.when(both(exists, jnp.logical_not(short)))
        def _():
            getattr(hop(t, up, level, which, step, k, False), verb)()

    def chain_step(t, step):
        for k in range(group):
            which = (g + group - k) % group
            if step == 0:
                if k == 0:
                    locals_[t].wait()
                else:
                    hop(t, 1, z, which, step, k, False).wait_recv()
                push(t, 1, z, which, step, k, "start")
                push(t, 0, z, which, step, k, "start")
                continue

            @pl.when(z >= step)
            def _():
                @pl.when(is_end)
                def _():
                    hop(t, 1, z - step, which, step, k, True).wait_recv()

                @pl.when(is_inner)
                def _():
                    hop(t, 1, z - step, which, step, k, False).wait_recv()

                push(t, 1, z - step, which, step, k, "start")

            @pl.when(z + step < layers)
            def _():
                @pl.when(is_end)
                def _():
                    hop(t, 0, z + step, which, step, k, True).wait_recv()

                @pl.when(is_inner)
                def _():
                    hop(t, 0, z + step, which, step, k, False).wait_recv()

                push(t, 0, z + step, which, step, k, "start")

    def chain_drain(t):
        for step in range(layers):
            for k in range(group):
                which = (g + group - k) % group

                @pl.when(z >= step)
                def _():
                    push(t, 1, z - step, which, step, k, "wait_send")

                @pl.when(z + step < layers)
                def _():
                    push(t, 0, z + step, which, step, k, "wait_send")

    def every(buf, field, far):
        if far:
            return buf[:, :, field, :, held:].reshape(count, spare)
        return buf[:, :, field, :, :held].reshape(count, held)

    def one(level, field, far):
        if far:
            return m_all[level, :, field, :, held:].reshape(slab, spare)
        return m_all[level, :, field, :, :held].reshape(slab, held)

    contract = (((1,), (1,)), ((), ()))

    def inner_product(left, right):
        return lax.dot_general(left, right, contract, preferred_element_type=jnp.float32)

    for step in range(layers):
        chain_step(0, step)
    chain_step(1, 0)

    gram = jnp.zeros((slab, count), jnp.float32)
    for field in range(fields):
        gram += inner_product(one(z, field, False), every(m_all, field, False))
    part[:, :piece, :] = gram.reshape(peers, piece, count)

    @pl.when(is_inner)
    def _():
        own = jnp.zeros((slab, count), jnp.float32)
        other = jnp.zeros((slab, count), jnp.float32)
        squares = jnp.zeros((8, count), jnp.float32)
        for field in range(fields):
            far = every(m_all, field, True)
            own += inner_product(one(z, field, True), far)
            other += inner_product(one(mate, field, True), far)
            for block in (every(m_all, field, False), far):
                ones = jnp.ones((8, block.shape[1]), jnp.bfloat16)
                wide = block.astype(jnp.float32)
                wide = wide * wide
                high = wide.astype(jnp.bfloat16)
                low = (wide - high.astype(jnp.float32)).astype(jnp.bfloat16)
                squares += inner_product(ones, high)
                squares += inner_product(ones, low)
        part[:, :piece, :] += own.reshape(peers, piece, count)
        part[:, piece:2 * piece, :] = other.reshape(peers, piece, count)
        part[:, 2 * piece:, :] = jnp.broadcast_to(squares[None], (peers, 8, count))

    def rs_copy(to, slot, k, inner):
        span = pl.ds(0, 2 * piece + 8 if inner else piece)
        return pltpu.make_async_remote_copy(
            src_ref=part.at[to, span],
            dst_ref=inbox.at[slot, span],
            send_sem=rs_send.at[k],
            recv_sem=rs_recv.at[slot],
            device_id=layer_id(to),
            device_id_type=MESH,
        )

    def swap(inner):
        span = pl.ds(0, piece + 8 if inner else piece)
        return pltpu.make_async_remote_copy(
            src_ref=swap_out.at[span],
            dst_ref=swap_in.at[span],
            send_sem=swap_sem.at[0],
            recv_sem=swap_sem.at[1],
            device_id=(mate * group + g, y),
            device_id_type=MESH,
        )

    def k_copy(half, to, slot, k):
        return pltpu.make_async_remote_copy(
            src_ref=krows.at[half, slot],
            dst_ref=krows.at[half, slot],
            send_sem=k_send.at[half, k],
            recv_sem=k_recv.at[half, slot],
            device_id=layer_id(to),
            device_id_type=MESH,
        )

    scale = scale_ref[0]

    def make_rows(half, level, row_gram, row_squares):
        first = level * slab + me * piece
        row_index = lax.broadcasted_iota(jnp.int32, (piece, count), 0) + first
        col_index = lax.broadcasted_iota(jnp.int32, (piece, count), 1)
        own_squares = jnp.sum(
            jnp.where(row_index == col_index, row_gram, 0.0), axis=1, keepdims=True
        )
        distance = own_squares + row_squares - 2.0 * row_gram
        divisor = jnp.full((piece, count), scale * total_cells, jnp.float32)
        krows[half, me] = jnp.exp(-distance / divisor).astype(jnp.bfloat16)
        for k in range(1, peers):
            k_copy(half, (me + k) % peers, me, k).start()

    def rs_start(inner):
        for k in range(1, peers):
            rs_copy((me + k) % peers, me, k, inner).start()

    def rs_finish(inner):
        for k in range(1, peers):
            source = (me + peers - k) % peers
            rs_copy(source, source, k, inner).wait_recv()
        span = slice(0, 2 * piece + 8 if inner else piece)
        inbox[me, span] = part[me, span]
        total = inbox[0, span]
        for k in range(1, peers):
            total = total + inbox[k, span]
        return total

    @pl.when(is_end)
    def _():
        rs_start(False)
        chain_step(1, 1)
        total = rs_finish(False)
        swap_out[:piece] = total
        swap(False).start()
        swap(True).wait_recv()
        make_rows(0, z, total + swap_in[:piece], swap_in[piece:piece + 1])
        chain_step(1, 2)

    @pl.when(is_inner)
    def _():
        rs_start(True)
        chain_step(1, 1)
        total = rs_finish(True)
        swap_out[...] = total[piece:]
        swap(True).start()
        make_rows(0, z, total[:piece], total[2 * piece:2 * piece + 1])
        chain_step(1, 2)
        swap(False).wait_recv()
        make_rows(1, mate, total[piece:2 * piece] + swap_in[:piece], total[2 * piece:2 * piece + 1])

    def k_wait(half):
        for k in range(1, peers):
            source = (me + peers - k) % peers
            k_copy(half, source, source, k).wait_recv()

    def rowsum_of(kernel):
        return jnp.sum(kernel.astype(jnp.float32), axis=1, keepdims=True)

    def pulled_term(kernel, level, field, far):
        own = one(level, field, far).astype(jnp.float32)
        pulled = jnp.dot(kernel, every(m_all, field, far), preferred_element_type=jnp.float32)
        factor = 2.0 / jnp.full(own.shape, scale, jnp.float32)
        return factor * (rowsum_of(kernel) * own - pulled)

    def attract_term(kernel, field, far):
        return jnp.dot(kernel, every(g_all, field, far), preferred_element_type=jnp.float32)

    k_wait(0)
    kernel = krows[0].reshape(slab, count)
    for field in range(fields):
        base[field, :, :held] = pulled_term(kernel, z, field, False)

    @pl.when(is_inner)
    def _():
        k_wait(1)
        mine = krows[0].reshape(slab, count)
        theirs = krows[1].reshape(slab, count)
        for field in range(fields):
            base[field, :, held:] = pulled_term(mine, z, field, True)
            base_far[field] = pulled_term(theirs, mate, field, True)

    chain_step(1, 3)

    def far_copy(field, to, source):
        return pltpu.make_async_remote_copy(
            src_ref=outbox_far.at[field, to],
            dst_ref=out_ref.at[field, :, columns(source, held, spare)],
            send_sem=o_send.at[1, field, to],
            recv_sem=o_recv.at[1, field, source],
            device_id=(mate * group + to, y),
            device_id_type=MESH,
        )

    def out_copy(field, to, source, inner):
        size = cells if inner else held
        return pltpu.make_async_remote_copy(
            src_ref=outbox.at[field, to, :, pl.ds(0, size)],
            dst_ref=out_ref.at[field, :, columns(source, 0, size)],
            send_sem=o_send.at[0, field, to],
            recv_sem=o_recv.at[0, field, source],
            device_id=(z * group + to, y),
            device_id_type=MESH,
        )

    for field in range(fields):
        @pl.when(is_inner)
        def _():
            mine = krows[0].reshape(slab, count)
            theirs = krows[1].reshape(slab, count)
            update = (attract_term(theirs, field, True) + base_far[field]) * (1.0 / count)
            outbox_far[field] = update.reshape(group, rows, spare)
            for to in range(group):
                far_copy(field, to, g).start()
            update = (attract_term(mine, field, True) + base[field, :, held:]) * (1.0 / count)
            outbox[field, :, :, held:] = update.reshape(group, rows, spare)

        update = (attract_term(kernel, field, False) + base[field, :, :held]) * (1.0 / count)
        outbox[field, :, :, :held] = update.reshape(group, rows, held)

        @pl.when(is_inner)
        def _():
            for k in range(1, group):
                out_copy(field, (g + k) % group, g, True).start()
            out_ref[field, :, columns(g)] = outbox[field, g]

        @pl.when(is_end)
        def _():
            for k in range(1, group):
                out_copy(field, (g + k) % group, g, False).start()
            out_ref[field, :, columns(g, 0, held)] = outbox[field, g, :, :held]

    chain_drain(0)
    chain_drain(1)
    for copy in pending:
        copy.wait_send()

    @pl.when(is_inner)
    def _():
        for k in range(1, peers):
            rs_copy((me + k) % peers, me, k, True).wait_send()
            k_copy(0, (me + k) % peers, me, k).wait_send()
            k_copy(1, (me + k) % peers, me, k).wait_send()
        swap(True).wait_send()
        for field in range(fields):
            for k in range(1, group):
                out_copy(field, (g + k) % group, g, True).wait_send()
                source = (g + group - k) % group
                out_copy(field, source, source, True).wait_recv()
            for to in range(group):
                far_copy(field, to, g).wait_send()

    @pl.when(is_end)
    def _():
        for k in range(1, peers):
            rs_copy((me + k) % peers, me, k, False).wait_send()
            k_copy(0, (me + k) % peers, me, k).wait_send()
        swap(False).wait_send()
        for field in range(fields):
            for k in range(1, group):
                out_copy(field, (g + k) % group, g, False).wait_send()
                source = (g + group - k) % group
                out_copy(field, source, source, False).wait_recv()
            for source in range(group):
                far_copy(field, source, source).wait_recv()


def fused_body(layers, group, planes, models, gradients, length_scale):
    fields, rows, width = models.shape
    cells = width // group
    slab = group * rows
    count = layers * slab
    peers = group * planes
    piece = slab // peers
    held = cells * 3 // 4
    dma = pltpu.SemaphoreType.DMA
    return pl.pallas_call(
        functools.partial(stein_kernel, layers, group, planes, held),
        out_shape=jax.ShapeDtypeStruct(models.shape, jnp.float32),
        in_specs=[
            pl.BlockSpec(memory_space=pltpu.SMEM),
            pl.BlockSpec(memory_space=pl.ANY),
            pl.BlockSpec(memory_space=pl.ANY),
        ],
        out_specs=pl.BlockSpec(memory_space=pltpu.VMEM),
        scratch_shapes=[
            pltpu.VMEM((layers, group, fields, rows, cells), jnp.bfloat16),
            pltpu.VMEM((layers, group, fields, rows, cells), jnp.bfloat16),
            pltpu.VMEM((peers, 2 * piece + 8, count), jnp.float32),
            pltpu.VMEM((peers, 2 * piece + 8, count), jnp.float32),
            pltpu.VMEM((piece + 8, count), jnp.float32),
            pltpu.VMEM((piece + 8, count), jnp.float32),
            pltpu.VMEM((2, peers, piece, count), jnp.bfloat16),
            pltpu.VMEM((fields, slab, cells), jnp.float32),
            pltpu.VMEM((fields, slab, cells - held), jnp.float32),
            pltpu.VMEM((fields, group, rows, cells), jnp.float32),
            pltpu.VMEM((fields, group, rows, cells - held), jnp.float32),
            dma((2,)),
            dma((2, group)),
            dma((layers, group)),
            dma((layers, group)),
            dma((2, 2, layers, group)),
            dma((peers,)),
            dma((peers,)),
            dma((2,)),
            dma((2, peers)),
            dma((2, peers)),
            dma((2, fields, group)),
            dma((2, fields, group)),
        ],
        compiler_params=pltpu.CompilerParams(collective_id=0, has_side_effects=True),
        name="stein",
    )(length_scale, models, gradients)


def solution(mesh):
    spread, planes = mesh.shape["dom"], mesh.shape["cell"]
    layers = math.isqrt(spread)
    group = spread // layers

    def body(models, gradients, length_scale):
        _, rows, width = models.shape
        fits = (
            layers == 4
            and layers * group == spread
            and width % (group * 512) == 0
            and rows % 16 == 0
            and (group * rows) % (group * planes * 16) == 0
        )
        if not fits:
            return plain_body(models, gradients, length_scale)
        return fused_body(layers, group, planes, models, gradients, length_scale)

    placed = (P(None, "dom", "cell"), P(None, "dom", "cell"), P())
    return jax.shard_map(
        body, mesh=mesh, in_specs=placed, out_specs=P(None, "dom", "cell"), check_vma=False
    )
```

time: 55.4 us -> 50.4 us (0.910)
  Pallas kernels: 52.7 us -> 47.7 us
    pallas_call x1, Pallas kernels: 52.7 us -> 47.7 us  [fused_body(): pl.pallas_call(functools.partial(stein_kernel, layers, group, planes, hel...]
where the time goes in v2:
time: 50.4 us; the launch traced here: 50.2 us
  Pallas kernels  47.7 us (95%)
  local copies, waits for them, and re-layouts  1.87 us (4%)
  between operations  0.66 us (1%)
    pallas_call x1, Pallas kernels, fused_body(): pl.pallas_call(functools.partial(stein_kernel, layers, group, planes, hel...  47.7 us
    unnamed x1, local copies, waits for them, and re-layouts  1.87 us

profile of v2, /device:TPU:0, one launch (start us, length us, event | category | flops | bytes accessed | tf_op | source)
XLA Modules:
  0.0 50.2 jit_solution(18142095878725655737)
XLA Ops:
  0.7 47.7 %stein.1 = f32[2,32,2048]{2,1,0:T(8,128)} custom-call(f32[1]{0:T(128)S(6)} %copy.5.scale_ref, bf16[2,32,2048]{2,1,0:T(8,128)(2,1)} %models_ref.1, bf16[2,32,2048]{2,1,0:T(8,128)(2,1)} %grads_ref.1), custom_call_target="tpu_custom_call" | custom-call | tf_op jit(solution)/shard_map/stein/pallas_call | solution.py:462
  48.4 1.9 %copy.6 = f32[2,32,2048]{2,1,0:T(8,128)} copy(f32[2,32,2048]{2,1,0:T(8,128)} %stein.1) | data formatting | bytes 1048576

commit v3 on v2

--- a/solution.py
+++ b/solution.py
@@ -219,46 +219,85 @@
     def inner_product(left, right):
         return lax.dot_general(left, right, contract, preferred_element_type=jnp.float32)
 
-    for step in range(layers):
-        chain_step(0, step)
-    chain_step(1, 0)
-
-    gram = jnp.zeros((slab, count), jnp.float32)
-    for field in range(fields):
-        gram += inner_product(one(z, field, False), every(m_all, field, False))
-    part[:, :piece, :] = gram.reshape(peers, piece, count)
-
-    @pl.when(is_inner)
-    def _():
-        own = jnp.zeros((slab, count), jnp.float32)
-        other = jnp.zeros((slab, count), jnp.float32)
-        squares = jnp.zeros((8, count), jnp.float32)
-        for field in range(fields):
-            far = every(m_all, field, True)
-            own += inner_product(one(z, field, True), far)
-            other += inner_product(one(mate, field, True), far)
-            for block in (every(m_all, field, False), far):
-                ones = jnp.ones((8, block.shape[1]), jnp.bfloat16)
-                wide = block.astype(jnp.float32)
-                wide = wide * wide
-                high = wide.astype(jnp.bfloat16)
-                low = (wide - high.astype(jnp.float32)).astype(jnp.bfloat16)
-                squares += inner_product(ones, high)
-                squares += inner_product(ones, low)
-        part[:, :piece, :] += own.reshape(peers, piece, count)
-        part[:, piece:2 * piece, :] = other.reshape(peers, piece, count)
-        part[:, 2 * piece:, :] = jnp.broadcast_to(squares[None], (peers, 8, count))
-
-    def rs_copy(to, slot, k, inner):
+    def block_of(buf, level, field, far):
+        if far:
+            return buf[level, :, field, :, held:].reshape(slab, spare)
+        return buf[level, :, field, :, :held].reshape(slab, held)
+
+    def rs_copy(level, to, slot, k, inner):
         span = pl.ds(0, 2 * piece + 8 if inner else piece)
         return pltpu.make_async_remote_copy(
-            src_ref=part.at[to, span],
-            dst_ref=inbox.at[slot, span],
-            send_sem=rs_send.at[k],
-            recv_sem=rs_recv.at[slot],
+            src_ref=part.at[level, to, span],
+            dst_ref=inbox.at[level, slot, span],
+            send_sem=rs_send.at[level, k],
+            recv_sem=rs_recv.at[level, slot],
             device_id=layer_id(to),
             device_id_type=MESH,
         )
+
+    def gram_level(level):
+        own = jnp.zeros((slab, slab), jnp.float32)
+        for field in range(fields):
+            own += inner_product(one(z, field, False), block_of(m_all, level, field, False))
+        part[level, :, :piece, :] = own.reshape(peers, piece, slab)
+
+        @pl.when(is_inner)
+        def _():
+            mine = jnp.zeros((slab, slab), jnp.float32)
+            other = jnp.zeros((slab, slab), jnp.float32)
+            squares = jnp.zeros((8, slab), jnp.float32)
+            for field in range(fields):
+                far = block_of(m_all, level, field, True)
+                mine += inner_product(one(z, field, True), far)
+                other += inner_product(one(mate, field, True), far)
+                for block in (block_of(m_all, level, field, False), far):
+                    ones = jnp.ones((8, block.shape[1]), jnp.bfloat16)
+                    wide = block.astype(jnp.float32)
+                    wide = wide * wide
+                    high = wide.astype(jnp.bfloat16)
+                    low = (wide - high.astype(jnp.float32)).astype(jnp.bfloat16)
+                    squares += inner_product(ones, high)
+                    squares += inner_product(ones, low)
+            part[level, :, :piece, :] += mine.reshape(peers, piece, slab)
+            part[level, :, piece:2 * piece, :] = other.reshape(peers, piece, slab)
+            part[level, :, 2 * piece:, :] = jnp.broadcast_to(squares[None], (peers, 8, slab))
+            for k in range(1, peers):
+                rs_copy(level, (me + k) % peers, me, k, True).start()
+            inbox[level, me] = part[level, me]
+
+        @pl.when(is_end)
+        def _():
+            for k in range(1, peers):
+                rs_copy(level, (me + k) % peers, me, k, False).start()
+            inbox[level, me, :piece] = part[level, me, :piece]
+
+    def gram_step(step):
+        @pl.when(z >= step)
+        def _():
+            gram_level(z - step)
+
+        @pl.when(z + step < layers)
+        def _():
+            gram_level(z + step)
+
+    chain_step(0, 0)
+
+    @pl.when(is_end)
+    def _():
+        chain_step(1, 0)
+
+    chain_step(0, 1)
+    gram_level(z)
+    gram_step(1)
+    chain_step(0, 2)
+
+    @pl.when(is_inner)
+    def _():
+        chain_step(1, 0)
+
+    gram_step(2)
+    chain_step(0, 3)
+    gram_step(3)
 
     def swap(inner):
         span = pl.ds(0, piece + 8 if inner else piece)
@@ -296,24 +335,21 @@
         for k in range(1, peers):
             k_copy(half, (me + k) % peers, me, k).start()
 
-    def rs_start(inner):
-        for k in range(1, peers):
-            rs_copy((me + k) % peers, me, k, inner).start()
-
     def rs_finish(inner):
-        for k in range(1, peers):
-            source = (me + peers - k) % peers
-            rs_copy(source, source, k, inner).wait_recv()
         span = slice(0, 2 * piece + 8 if inner else piece)
-        inbox[me, span] = part[me, span]
-        total = inbox[0, span]
-        for k in range(1, peers):
-            total = total + inbox[k, span]
-        return total
+        totals = []
+        for level in range(layers):
+            for k in range(1, peers):
+                source = (me + peers - k) % peers
+                rs_copy(level, source, source, k, inner).wait_recv()
+            total = inbox[level, 0, span]
+            for k in range(1, peers):
+                total = total + inbox[level, k, span]
+            totals.append(total)
+        return jnp.concatenate(totals, axis=1)
 
     @pl.when(is_end)
     def _():
-        rs_start(False)
         chain_step(1, 1)
         total = rs_finish(False)
         swap_out[:piece] = total
@@ -324,7 +360,6 @@
 
     @pl.when(is_inner)
     def _():
-        rs_start(True)
         chain_step(1, 1)
         total = rs_finish(True)
         swap_out[...] = total[piece:]
@@ -423,7 +458,8 @@
     @pl.when(is_inner)
     def _():
         for k in range(1, peers):
-            rs_copy((me + k) % peers, me, k, True).wait_send()
+            for level in range(layers):
+                rs_copy(level, (me + k) % peers, me, k, True).wait_send()
             k_copy(0, (me + k) % peers, me, k).wait_send()
             k_copy(1, (me + k) % peers, me, k).wait_send()
         swap(True).wait_send()
@@ -438,7 +474,8 @@
     @pl.when(is_end)
     def _():
         for k in range(1, peers):
-            rs_copy((me + k) % peers, me, k, False).wait_send()
+            for level in range(layers):
+                rs_copy(level, (me + k) % peers, me, k, False).wait_send()
             k_copy(0, (me + k) % peers, me, k).wait_send()
         swap(False).wait_send()
         for field in range(fields):
@@ -457,7 +494,7 @@
     count = layers * slab
     peers = group * planes
     piece = slab // peers
-    held = cells * 3 // 4
+    held = cells // 2
     dma = pltpu.SemaphoreType.DMA
     return pl.pallas_call(
         functools.partial(stein_kernel, layers, group, planes, held),
@@ -471,8 +508,8 @@
         scratch_shapes=[
             pltpu.VMEM((layers, group, fields, rows, cells), jnp.bfloat16),
             pltpu.VMEM((layers, group, fields, rows, cells), jnp.bfloat16),
-            pltpu.VMEM((peers, 2 * piece + 8, count), jnp.float32),
-            pltpu.VMEM((peers, 2 * piece + 8, count), jnp.float32),
+            pltpu.VMEM((layers, peers, 2 * piece + 8, slab), jnp.float32),
+            pltpu.VMEM((layers, peers, 2 * piece + 8, slab), jnp.float32),
             pltpu.VMEM((piece + 8, count), jnp.float32),
             pltpu.VMEM((piece + 8, count), jnp.float32),
             pltpu.VMEM((2, peers, piece, count), jnp.bfloat16),
@@ -485,8 +522,8 @@
             dma((layers, group)),
             dma((layers, group)),
             dma((2, 2, layers, group)),
-            dma((peers,)),
-            dma((peers,)),
+            dma((layers, peers)),
+            dma((layers, peers)),
             dma((2,)),
             dma((2, peers)),
             dma((2, peers)),
@@ -510,6 +547,7 @@
             and layers * group == spread
             and width % (group * 512) == 0
             and rows % 16 == 0
+            and (group * rows) % 128 == 0
             and (group * rows) % (group * planes * 16) == 0
         )
         if not fits:

time: 50.4 us -> 48.5 us (0.962)
  Pallas kernels: 47.7 us -> 45.8 us
    pallas_call x1, Pallas kernels: 47.7 us -> 45.8 us  [fused_body(): pl.pallas_call(functools.partial(stein_kernel, layers, group, planes, hel...]
where the time goes in v3:
time: 48.5 us; the launch traced here: 48.3 us
  Pallas kernels  45.8 us (94%)
  local copies, waits for them, and re-layouts  1.87 us (4%)
  between operations  0.66 us (1%)
    pallas_call x1, Pallas kernels, fused_body(): pl.pallas_call(functools.partial(stein_kernel, layers, group, planes, hel...  45.8 us
    unnamed x1, local copies, waits for them, and re-layouts  1.87 us

profile of v3, /device:TPU:0, one launch (start us, length us, event | category | flops | bytes accessed | tf_op | source)
XLA Modules:
  0.0 48.3 jit_solution(12028939406140306936)
XLA Ops:
  0.7 45.8 %stein.1 = f32[2,32,2048]{2,1,0:T(8,128)} custom-call(f32[1]{0:T(128)S(6)} %copy.5.scale_ref, bf16[2,32,2048]{2,1,0:T(8,128)(2,1)} %models_ref.1, bf16[2,32,2048]{2,1,0:T(8,128)(2,1)} %grads_ref.1), custom_call_target="tpu_custom_call" | custom-call | tf_op jit(solution)/shard_map/stein/pallas_call | solution.py:499
  46.4 1.9 %copy.6 = f32[2,32,2048]{2,1,0:T(8,128)} copy(f32[2,32,2048]{2,1,0:T(8,128)} %stein.1) | data formatting | bytes 1048576

commit v4 on v3

--- a/solution.py
+++ b/solution.py
@@ -49,8 +49,8 @@
 def stein_kernel(
     layers, group, planes, held,
     scale_ref, models_ref, grads_ref, out_ref,
-    m_all, g_all, part, inbox, swap_out, swap_in, krows, base, base_far, outbox, outbox_far,
-    local_sem, a2a_send, m_recv, g_recv, fwd_send,
+    m_all, g_zero, g_one, part, inbox, swap_out, swap_in, krows, base, base_far, outbox, outbox_far,
+    local_sem, a2a_send, chain_recv, fwd_send,
     rs_send, rs_recv, swap_sem, k_send, k_recv, o_send, o_recv,
 ):
     fields, rows, width = models_ref.shape
@@ -105,11 +105,21 @@
     def _():
         pl.semaphore_signal(barrier, inc=1, device_id=(dom - group, y), device_id_type=MESH)
 
-    tensors = ((models_ref, m_all, m_recv), (grads_ref, g_all, g_recv))
+    tensors = (
+        (models_ref, m_all, chain_recv.at[0]),
+        (grads_ref.at[0], g_zero, chain_recv.at[1]),
+        (grads_ref.at[1], g_one, chain_recv.at[2]),
+    )
+
+    def strip(ref, span):
+        if len(ref.shape) == 3:
+            return ref.at[:, :, span]
+        return ref.at[:, span]
+
     locals_ = []
     for t, (src, dst, _) in enumerate(tensors):
         copy = pltpu.make_async_copy(
-            src.at[:, :, columns(g)], dst.at[z, g], local_sem.at[t]
+            strip(src, columns(g)), dst.at[z, g], local_sem.at[t]
         )
         copy.start()
         locals_.append(copy)
@@ -122,7 +132,7 @@
         for k in range(1, group):
             to = (g + k) % group
             copy = pltpu.make_async_remote_copy(
-                src_ref=src.at[:, :, columns(to)],
+                src_ref=strip(src, columns(to)),
                 dst_ref=dst.at[z, g],
                 send_sem=a2a_send.at[t, k],
                 recv_sem=recv.at[z, g],
@@ -134,7 +144,7 @@
 
     def hop(t, up, level, which, step, k, short):
         _, buf, recv = tensors[t]
-        block = buf.at[level, which, :, :, near] if short else buf.at[level, which]
+        block = strip(buf.at[level, which], near) if short else buf.at[level, which]
         return pltpu.make_async_remote_copy(
             src_ref=block,
             dst_ref=block,
@@ -285,6 +295,7 @@
     @pl.when(is_end)
     def _():
         chain_step(1, 0)
+        chain_step(2, 0)
 
     chain_step(0, 1)
     gram_level(z)
@@ -350,17 +361,16 @@
 
     @pl.when(is_end)
     def _():
-        chain_step(1, 1)
         total = rs_finish(False)
         swap_out[:piece] = total
         swap(False).start()
         swap(True).wait_recv()
         make_rows(0, z, total + swap_in[:piece], swap_in[piece:piece + 1])
-        chain_step(1, 2)
 
     @pl.when(is_inner)
     def _():
         chain_step(1, 1)
+        chain_step(2, 0)
         total = rs_finish(True)
         swap_out[...] = total[piece:]
         swap(True).start()
@@ -368,6 +378,7 @@
         chain_step(1, 2)
         swap(False).wait_recv()
         make_rows(1, mate, total[piece:2 * piece] + swap_in[:piece], total[2 * piece:2 * piece + 1])
+        chain_step(2, 1)
 
     def k_wait(half):
         for k in range(1, peers):
@@ -384,7 +395,10 @@
         return factor * (rowsum_of(kernel) * own - pulled)
 
     def attract_term(kernel, field, far):
-        return jnp.dot(kernel, every(g_all, field, far), preferred_element_type=jnp.float32)
+        buf = (g_zero, g_one)[field]
+        block = buf[..., held:] if far else buf[..., :held]
+        block = block.reshape(count, block.shape[-1])
+        return jnp.dot(kernel, block, preferred_element_type=jnp.float32)
 
     k_wait(0)
     kernel = krows[0].reshape(slab, count)
@@ -399,8 +413,6 @@
         for field in range(fields):
             base[field, :, held:] = pulled_term(mine, z, field, True)
             base_far[field] = pulled_term(theirs, mate, field, True)
-
-    chain_step(1, 3)
 
     def far_copy(field, to, source):
         return pltpu.make_async_remote_copy(
@@ -424,6 +436,16 @@
         )
 
     for field in range(fields):
+        @pl.when(is_end)
+        def _():
+            for step in range(1, layers):
+                chain_step(1 + field, step)
+
+        if field == 1:
+            @pl.when(is_inner)
+            def _():
+                chain_step(2, 2)
+
         @pl.when(is_inner)
         def _():
             mine = krows[0].reshape(slab, count)
@@ -452,6 +474,7 @@
 
     chain_drain(0)
     chain_drain(1)
+    chain_drain(2)
     for copy in pending:
         copy.wait_send()
 
@@ -507,7 +530,8 @@
         out_specs=pl.BlockSpec(memory_space=pltpu.VMEM),
         scratch_shapes=[
             pltpu.VMEM((layers, group, fields, rows, cells), jnp.bfloat16),
-            pltpu.VMEM((layers, group, fields, rows, cells), jnp.bfloat16),
+            pltpu.VMEM((layers, group, rows, cells), jnp.bfloat16),
+            pltpu.VMEM((layers, group, rows, cells), jnp.bfloat16),
             pltpu.VMEM((layers, peers, 2 * piece + 8, slab), jnp.float32),
             pltpu.VMEM((layers, peers, 2 * piece + 8, slab), jnp.float32),
             pltpu.VMEM((piece + 8, count), jnp.float32),
@@ -517,11 +541,10 @@
             pltpu.VMEM((fields, slab, cells - held), jnp.float32),
             pltpu.VMEM((fields, group, rows, cells), jnp.float32),
             pltpu.VMEM((fields, group, rows, cells - held), jnp.float32),
-            dma((2,)),
-            dma((2, group)),
-            dma((layers, group)),
-            dma((layers, group)),
-            dma((2, 2, layers, group)),
+            dma((3,)),
+            dma((3, group)),
+            dma((3, layers, group)),
+            dma((3, 2, layers, group)),
             dma((layers, peers)),
             dma((layers, peers)),
             dma((2,)),
@@ -544,6 +567,7 @@
         _, rows, width = models.shape
         fits = (
             layers == 4
+            and models.shape[0] == 2
             and layers * group == spread
             and width % (group * 512) == 0
             and rows % 16 == 0

time: 48.5 us -> 49.6 us (1.023)
  Pallas kernels: 45.8 us -> 46.9 us
    pallas_call x1, Pallas kernels: 45.8 us -> 46.9 us  [fused_body(): pl.pallas_call(functools.partial(stein_kernel, layers, group, planes, hel...]
where the time goes in v4:
time: 49.6 us; the launch traced here: 49.4 us
  Pallas kernels  46.9 us (95%)
  local copies, waits for them, and re-layouts  1.87 us (4%)
  between operations  0.66 us (1%)
    pallas_call x1, Pallas kernels, fused_body(): pl.pallas_call(functools.partial(stein_kernel, layers, group, planes, hel...  46.9 us
    unnamed x1, local copies, waits for them, and re-layouts  1.87 us

profile of v4, /device:TPU:0, one launch (start us, length us, event | category | flops | bytes accessed | tf_op | source)
XLA Modules:
  0.0 49.4 jit_solution(13816165910400224853)
XLA Ops:
  0.7 46.9 %stein.1 = f32[2,32,2048]{2,1,0:T(8,128)} custom-call(f32[1]{0:T(128)S(6)} %copy.5.scale_ref, bf16[2,32,2048]{2,1,0:T(8,128)(2,1)} %models_ref.1, bf16[2,32,2048]{2,1,0:T(8,128)(2,1)} %grads_ref.1), custom_call_target="tpu_custom_call" | custom-call | tf_op jit(solution)/shard_map/stein/pallas_call | solution.py:522
  47.5 1.9 %copy.6 = f32[2,32,2048]{2,1,0:T(8,128)} copy(f32[2,32,2048]{2,1,0:T(8,128)} %stein.1) | data formatting | bytes 1048576

commit v5 on v4

--- a/solution.py
+++ b/solution.py
@@ -441,7 +441,7 @@
             for step in range(1, layers):
                 chain_step(1 + field, step)
 
-        if field == 1:
+        if field == 0:
             @pl.when(is_inner)
             def _():
                 chain_step(2, 2)

time: 49.6 us -> 47.4 us (0.956)
  Pallas kernels: 46.9 us -> 44.7 us
    pallas_call x1, Pallas kernels: 46.9 us -> 44.7 us  [fused_body(): pl.pallas_call(functools.partial(stein_kernel, layers, group, planes, hel...]
where the time goes in v5:
time: 47.4 us; the launch traced here: 47.2 us
  Pallas kernels  44.7 us (94%)
  local copies, waits for them, and re-layouts  1.87 us (4%)
  between operations  0.66 us (1%)
    pallas_call x1, Pallas kernels, fused_body(): pl.pallas_call(functools.partial(stein_kernel, layers, group, planes, hel...  44.7 us
    unnamed x1, local copies, waits for them, and re-layouts  1.87 us

profile of v5, /device:TPU:0, one launch (start us, length us, event | category | flops | bytes accessed | tf_op | source)
XLA Modules:
  0.0 47.2 jit_solution(2791108454531420549)
XLA Ops:
  0.7 44.7 %stein.1 = f32[2,32,2048]{2,1,0:T(8,128)} custom-call(f32[1]{0:T(128)S(6)} %copy.5.scale_ref, bf16[2,32,2048]{2,1,0:T(8,128)(2,1)} %models_ref.1, bf16[2,32,2048]{2,1,0:T(8,128)(2,1)} %grads_ref.1), custom_call_target="tpu_custom_call" | custom-call | tf_op jit(solution)/shard_map/stein/pallas_call | solution.py:522
  45.4 1.9 %copy.6 = f32[2,32,2048]{2,1,0:T(8,128)} copy(f32[2,32,2048]{2,1,0:T(8,128)} %stein.1) | data formatting | bytes 1048576
